TPU v7x, 32 devices: a whole 2x2x4 slice. The times are simulated.
32 devices in a mesh: rows: 8 (over z, x), col: 4 (over y, core).
Axes of the slice: x: 2, y: 2, z: 4, core: 2. Of those that a mesh axis runs over, the one named last changes fastest.
Arguments:
- factor_t: bfloat16 [112, 128, 128], P('rows', 'col'), may hold values from -0.25 to 1.25
- intersection_diag: bfloat16 [112, 128, 128], P('rows'), may hold values from -0.25 to 1.25
- intersection_near: bfloat16 [112, 3, 128, 128], P('rows'), may hold values from -0.3125 to 0.3125
- intersection_cross: bfloat16 [112, 4, 128, 128], P('rows'), may hold values from -0.3125 to 0.3125
- near_cols: int32 [112, 3], P('rows'), may hold values from 0 to 111, as said below
- cross_cols: int32 [112, 4], P('rows'), may hold values from 0 to 111, as said below
Outputs:
- refined_diag: bfloat16 [112, 128, 128], P('rows', 'col')
- refined_near: bfloat16 [112, 3, 128, 128], P('rows', None, 'col')
- refined_cross: bfloat16 [112, 4, 128, 128], P('rows', None, 'col')
Inputs may be any that keep to these rules, and one draw needn't show every extreme that they name: near_cols[i, k] differs from i by 1 to 14. cross_cols[i, k] lies in the other half of the block rows; the block rows i * 14 to i * 14 + 13 name at most 14 columns in any one group of 14 block rows, and some group is named that often.
All inputs are finite; a program needn't handle non-finite values.
Results may differ from a plain program's by a relative error of at most 0.0056.
Values may be sent and summed in bfloat16 or wider, within the bound.
A program may use at most 64 MiB of HBM per device.

v0:
```python
import functools

import jax
import jax.numpy as jnp
from jax import lax
from jax.experimental import pallas as pl
from jax.experimental.pallas import tpu as pltpu
from jax.sharding import PartitionSpec as P

F32 = jnp.float32
BF16 = jnp.bfloat16
LAG = 2
PARTS = 2
VMEM_LIMIT = 16 * 1024 * 1024
VMEM_ALL = 67043328
SLACK = 96 * 1024
NT = (((1,), (1,)), ((), ()))
TN = (((0,), (0,)), ((), ()))


def dot(a, b, dims=(((1,), (0,)), ((), ()))):
    return lax.dot_general(a, b, dims, preferred_element_type=F32)


def split(rows, parts):
    size = rows // parts
    return [pl.ds(p * size, size) for p in range(parts)]


def gather_kernel(
    n, c, parts, lag,
    factor, s_diag, s_near, s_cross,
    everyone, g, w_diag,
    full, v_diag, v_near, v_cross,
    load_sem, own_sem, col_send, col_recv, near_send, near_recv,
    first_send, slot_recv, second_send, third_send,
):
    per, width, order = factor.shape
    near, cross = v_near.shape[1], v_cross.shape[1]
    half = n // 2
    cut = [per * p // parts for p in range(parts + 1)]
    r = lax.axis_index("rows")
    q = lax.axis_index("col")
    upper = r // half
    m = r - upper * half
    my_base = upper * half
    other_base = (1 - upper) * half
    parity = m % 2
    mate = my_base + m + 1 - 2 * parity
    side = m - 1 + 2 * parity
    has_side = jnp.logical_and(side >= 0, side < half)
    partner = other_base + m
    cousins = [my_base + (m + 2 * k) % half for k in range(1, half // 2)]
    col_mate = q + 1 - 2 * (q % 2)
    col_cousins = [(q + 2 * k) % c for k in range(1, c // 2)]

    loads = [
        pltpu.make_async_copy(s_diag, v_diag, load_sem.at[0]),
        pltpu.make_async_copy(s_near, v_near, load_sem.at[1]),
        pltpu.make_async_copy(s_cross, v_cross, load_sem.at[2]),
    ]
    own_all = pltpu.make_async_copy(factor, everyone.at[pl.ds(r * per, per)], own_sem.at[0])

    def rows_of(column):
        return pl.ds(pl.multiple_of(column * width, width), width)

    own_full = pltpu.make_async_copy(factor, full.at[:, rows_of(q), :], own_sem.at[1])

    barrier = pltpu.get_barrier_semaphore()

    def greet(**where):
        pl.semaphore_signal(barrier, inc=1, device_id=where, device_id_type=pl.DeviceIdType.MESH)

    greet(rows=partner)
    greet(rows=mate)
    for cousin in cousins:
        greet(rows=cousin)
    greet(col=col_mate)
    for column in col_cousins:
        greet(col=column)

    @pl.when(has_side)
    def _():
        greet(rows=my_base + side)

    own_full.start()
    own_all.start()
    for load in loads:
        load.start()
    pl.semaphore_wait(barrier, 3 + len(cousins) + len(col_cousins) + has_side.astype(jnp.int32))

    def send(src, dst, send_sem, recv_sem, **where):
        return pltpu.make_async_remote_copy(
            src_ref=src, dst_ref=dst, send_sem=send_sem, recv_sem=recv_sem,
            device_id=where, device_id_type=pl.DeviceIdType.MESH,
        )

    sent = []

    def go(*args, **where):
        copy = send(*args, **where)
        copy.start()
        sent.append(copy)
        return copy

    for p in range(parts):
        go(
            factor.at[pl.ds(cut[p], cut[p + 1] - cut[p])],
            everyone.at[pl.ds(r * per + cut[p], cut[p + 1] - cut[p])],
            first_send.at[p], slot_recv.at[m, p], rows=partner,
        )
    halves = split(per, col_recv.shape[1])

    def column_piece(column, h):
        return full.at[halves[h], rows_of(column), :]

    for h in range(len(halves)):
        for k, column in enumerate(col_cousins):
            go(factor.at[halves[h]], column_piece(q, h), col_send.at[k, h], col_recv.at[q, h], col=column)
        go(factor.at[halves[h]], column_piece(q, h), col_send.at[len(col_cousins), h], col_recv.at[q, h], col=col_mate)
    mine = everyone.at[pl.ds(r * per, per)]
    to_mate = go(factor, mine, near_send.at[0], near_recv.at[0], rows=mate)
    to_side = send(factor, mine, near_send.at[1], near_recv.at[1], rows=my_base + side)

    @pl.when(has_side)
    def _():
        to_side.start()

    def slot(s, p):
        return everyone.at[pl.ds((other_base + s) * per + cut[p], cut[p + 1] - cut[p])]

    def arrive(s, p):
        send(slot(s, p), slot(s, p), first_send.at[p], slot_recv.at[s, p], rows=mate).wait_recv()

    def pass_on(s, p, send_sem, row):
        go(slot(s, p), slot(s, p), send_sem, slot_recv.at[s, p], rows=row)

    def arrive_column(column, h):
        ref = column_piece(column, h)
        send(ref, ref, col_send.at[0, h], col_recv.at[column, h], col=col_mate).wait_recv()

    eye = (
        lax.broadcasted_iota(jnp.int32, (width, order), 0) + q * width
        == lax.broadcasted_iota(jnp.int32, (width, order), 1)
    ).astype(F32)

    def prepare(i, carry):
        z_t = full[i]
        own = full[i, rows_of(q), :]
        square = (-0.5 * dot(z_t, z_t, TN)).astype(BF16)
        blocks = [v_near[i, k] for k in range(near)] + [v_cross[i, k] for k in range(cross)]
        wide = dot(square, jnp.concatenate(blocks, axis=1)).astype(BF16)
        for k in range(near + cross):
            g[i, k] = wide[:, k * order:(k + 1) * order]
        product = dot(own, v_diag[i], NT).astype(BF16)
        residual = (eye - dot(product, z_t, NT)).astype(BF16)
        w_diag[i] = (own.astype(F32) + 0.5 * dot(residual, z_t)).astype(BF16)
        return carry

    for t in range(parts + lag):
        if t < parts:
            arrive(m, t)
            for k, cousin in enumerate(cousins):
                pass_on(m, t, second_send.at[k, t], cousin)
            pass_on(m, t, third_send.at[0, t], mate)
        if 1 <= t <= len(halves):
            for k, column in enumerate(col_cousins):
                arrive_column(column, t - 1)
                ref = column_piece(column, t - 1)
                go(ref, ref, col_send.at[len(col_cousins) + 1 + k, t - 1], col_recv.at[column, t - 1], col=col_mate)
        if t == lag:
            own_full.wait()
            for load in loads:
                load.wait()
            for h in range(len(halves)):
                arrive_column(col_mate, h)
                for k in range(1, c // 2):
                    arrive_column((col_mate + 2 * k) % c, h)
        if t >= lag:
            for k in range(1, half // 2):
                s = (m + 2 * k) % half
                arrive(s, t - lag)
                pass_on(s, t - lag, third_send.at[k, t - lag], mate)
            lax.fori_loop(cut[t - lag], cut[t - lag + 1], prepare, 0, unroll=True)

    own_all.wait()
    to_mate.wait_recv()

    @pl.when(has_side)
    def _():
        to_side.wait_recv()

    for p in range(parts):
        for k in range(half // 2):
            arrive((m + 1 - 2 * parity + 2 * k) % half, p)

    for copy in sent:
        copy.wait_send()

    @pl.when(has_side)
    def _():
        to_side.wait_send()


def finish_kernel(
    near_cols, cross_cols, everyone, g, w_diag, o_diag, o_near, o_cross, w_near, w_cross, diag_sem, out_sem,
):
    per, near = w_near.shape[:2]
    cross = w_cross.shape[1]
    out_diag = pltpu.make_async_copy(w_diag, o_diag, diag_sem.at[0])
    out_diag.start()

    def outs(i):
        return (
            pltpu.make_async_copy(w_near.at[i], o_near.at[i], out_sem.at[0, i]),
            pltpu.make_async_copy(w_cross.at[i], o_cross.at[i], out_sem.at[1, i]),
        )

    def finish(i, carry):
        for k in range(near):
            w_near[i, k] = dot(everyone[near_cols[k, i]], g[i, k], NT).astype(BF16)
        for k in range(cross):
            w_cross[i, k] = dot(everyone[cross_cols[k, i]], g[i, near + k], NT).astype(BF16)
        for copy in outs(i):
            copy.start()
        return carry

    lax.fori_loop(0, per, finish, 0, unroll=True)
    out_diag.wait()

    def drain(i, carry):
        for copy in outs(i):
            copy.wait()
        return carry

    lax.fori_loop(0, per, drain, 0)


def body(n, c, factor_t, intersection_diag, intersection_near, intersection_cross, near_cols, cross_cols):
    per, width, order = factor_t.shape
    near, cross = near_cols.shape[1], cross_cols.shape[1]
    half = n // 2
    parts = min(PARTS, per)
    col_parts = 2 if per % 2 == 0 else 1
    smem = pl.BlockSpec(memory_space=pltpu.SMEM)
    vmem = pl.BlockSpec(memory_space=pltpu.VMEM)
    hbm = pl.BlockSpec(memory_space=pl.ANY)
    dma = pltpu.SemaphoreType.DMA
    kept = 2 * order * (n * per * width + per * (near + cross) * order + per * width)
    everyone, g, w_diag = pl.pallas_call(
        functools.partial(gather_kernel, n, c, parts, LAG),
        out_shape=(
            pltpu.VMEM((n * per, width, order), BF16),
            pltpu.VMEM((per, near + cross, order, order), BF16),
            pltpu.VMEM((per, width, order), BF16),
        ),
        in_specs=[pl.BlockSpec(memory_space=pltpu.HBM)] * 4,
        out_specs=(vmem, vmem, vmem),
        scratch_shapes=[
            pltpu.VMEM((per, order, order), BF16),
            pltpu.VMEM(intersection_diag.shape, BF16),
            pltpu.VMEM(intersection_near.shape, BF16),
            pltpu.VMEM(intersection_cross.shape, BF16),
            dma((3,)),
            dma((2,)),
            dma((c, col_parts)),
            dma((c, col_parts)),
            dma((2,)),
            dma((2,)),
            dma((parts,)),
            dma((half, parts)),
            dma((half // 2, parts)),
            dma((half // 2, parts)),
        ],
        compiler_params=pltpu.CompilerParams(
            collective_id=0, has_side_effects=True, vmem_limit_bytes=VMEM_ALL - kept - SLACK,
        ),
    )(factor_t, intersection_diag, intersection_near, intersection_cross)
    return pl.pallas_call(
        finish_kernel,
        out_shape=(
            jax.ShapeDtypeStruct((per, width, order), BF16),
            jax.ShapeDtypeStruct((per, near, width, order), BF16),
            jax.ShapeDtypeStruct((per, cross, width, order), BF16),
        ),
        in_specs=[smem, smem, vmem, vmem, vmem],
        out_specs=(hbm, hbm, hbm),
        scratch_shapes=[
            pltpu.VMEM((per, near, width, order), BF16),
            pltpu.VMEM((per, cross, width, order), BF16),
            dma((1,)),
            dma((2, per)),
        ],
        compiler_params=pltpu.CompilerParams(vmem_limit_bytes=VMEM_LIMIT),
    )(near_cols.T, cross_cols.T, everyone, g, w_diag)


def solution(mesh):
    placed = (
        P("rows", "col", None),
        P("rows", None, None),
        P("rows", None, None, None),
        P("rows", None, None, None),
        P("rows", None),
        P("rows", None),
    )
    return jax.shard_map(
        functools.partial(body, mesh.shape["rows"], mesh.shape["col"]),
        mesh=mesh,
        in_specs=placed,
        out_specs=(
            P("rows", "col", None),
            P("rows", None, "col", None),
            P("rows", None, "col", None),
        ),
        check_vma=False,
    )
```

profile of v0, /device:TPU:0, one launch (start us, length us, event | category | flops | bytes accessed | tf_op | source)
XLA Modules:
  0.0 23.2 jit_solution(4191868238834088089)
XLA Ops:
  0.6 0.0 copy-start
  0.6 0.0 copy-start.1
  0.7 19.3 %shard_map.85 = (bf16[112,32,128]{2,1,0:T(8,128)(2,1)S(1)}, bf16[14,7,128,128]{3,2,1,0:T(8,128)(2,1)S(1)}, bf16[14,32,128]{2,1,0:T(8,128)(2,1)S(1)}) custom-call(bf16[14,32,128]{2,1,0:T(8,128)(2,1)} %factor.1, bf16[14,128,128]{2,1,0:T(8,128)(2,1)} %s_diag.1, bf16[14,3,128,128]{3,2,1,0:T(8,128)(2,1)} %s_near.1, bf16[14,4,128,128]{3,2,1,0:T(8,128)(2,1)} %s_cross.1), custom_call_target="tpu_custom_call" | custom-call | tf_op jit(solution)/shard_map/pallas_call | solution.py:250
  19.9 0.0 copy-done
  19.9 0.0 copy-done.1
  20.0 3.3 %shard_map.86 = (bf16[14,32,128]{2,1,0:T(8,128)(2,1)}, bf16[14,3,32,128]{3,2,1,0:T(8,128)(2,1)}, bf16[14,4,32,128]{3,2,1,0:T(8,128)(2,1)}) custom-call(s32[3,14]{1,0:T(4,128)S(1)} %bitcast.2, s32[4,14]{1,0:T(4,128)S(1)} %bitcast.3, bf16[112,32,128]{2,1,0:T(8,128)(2,1)S(1)} %get-tuple-element.6.everyone, bf16[14,7,128,128]{3,2,1,0:T(8,128)(2,1)S(1)} %get-tuple-element.7.g, ...), custom_call_target="tpu_custom_call" | custom-call | tf_op jit(solution)/shard_map/pallas_call | solution.py:279
Async XLA Ops:
  0.6 19.3 %copy-start = (s32[14,3]{0,1:T(4,128)S(1)}, s32[14,3]{0,1:T(4,128)}, u32[]{:S(2)}) copy-start(s32[14,3]{0,1:T(4,128)} %param.10) | copy-start | bytes 508
  0.6 19.3 %copy-start.1 = (s32[14,4]{0,1:T(4,128)S(1)}, s32[14,4]{0,1:T(4,128)}, u32[]{:S(2)}) copy-start(s32[14,4]{0,1:T(4,128)} %param.11) | copy-start | bytes 676
where the time goes:
time: 23.4 us; the launch traced here: 23.2 us
  Pallas kernels  22.5 us (96%)
  between operations  0.67 us (3%)
    pallas_call x1, Pallas kernels, body(): pl.pallas_call(functools.partial(gather_kernel, n, c, parts, LAG), out_sh...  19.3 us
    pallas_call x1, Pallas kernels, body(): pl.pallas_call(finish_kernel, out_shape=(jax.ShapeDtypeStruct((per, width...  3.26 us

commit v1 on v0

v1 whole, which is shorter than its diff:
```python
import functools

import jax
import jax.numpy as jnp
from jax import lax
from jax.experimental import pallas as pl
from jax.experimental.pallas import tpu as pltpu
from jax.sharding import PartitionSpec as P

F32 = jnp.float32
BF16 = jnp.bfloat16
PARTS = 8
ROW_CUT = (0, 4, 8, 14)
VMEM_LIMIT = 16 * 1024 * 1024
VMEM_ALL = 67043328
SLACK = 96 * 1024
NT = (((1,), (1,)), ((), ()))
TN = (((0,), (0,)), ((), ()))


def dot(a, b, dims=(((1,), (0,)), ((), ()))):
    return lax.dot_general(a, b, dims, preferred_element_type=F32)


def split(rows, parts):
    size = rows // parts
    return [pl.ds(p * size, size) for p in range(parts)]


def refine_kernel(
    n, c, parts,
    factor, s_diag, s_near, s_cross, near_cols, cross_cols,
    w_diag, w_near, w_cross,
    everyone, nearby, g, full, v_diag, v_near, v_cross, near_at, cross_at,
    load_sem, own_sem, edge_sem, col_send, col_recv, near_send, near_recv,
    cross_send, outer_send, mate_send, chain_recv, mate_recv, ready,
):
    per, width, order = factor.shape
    near, cross = v_near.shape[1], v_cross.shape[1]
    half = n // 2
    planes = half // 2
    cut = [per * p // parts for p in range(parts + 1)]
    r = lax.axis_index("rows")
    q = lax.axis_index("col")
    upper = r // half
    is_upper = upper == 1
    m = r - upper * half
    s = m % 2
    d = jnp.where(is_upper, m // 2, planes - 1 - m // 2)
    inmost = d == 0
    beyond = d > 0
    lower_inmost = jnp.logical_and(upper == 0, inmost)
    upper_inmost = jnp.logical_and(is_upper, inmost)
    has_outer = d + 1 < planes
    mate = r + 1 - 2 * s
    target = jnp.where(is_upper, half - 2 + s, half + s)
    outer = jnp.where(is_upper, r + 2, r - 2)
    col_mate = q + 1 - 2 * (q % 2)
    col_cousins = [(q + 2 * k) % c for k in range(1, c // 2)]
    cousins = len(col_cousins)
    origin = jnp.logical_and(r == 0, q == 0)
    CORE, MATE, NEXT, CROSS, COUSIN = 0, 1, 2, 3, 4

    def other_row(e, side):
        return jnp.where(is_upper, half - 2 - 2 * e, half + 2 * e) + side

    loads = [
        pltpu.make_async_copy(s_diag, v_diag, load_sem.at[0]),
        pltpu.make_async_copy(s_near, v_near, load_sem.at[1]),
        pltpu.make_async_copy(s_cross, v_cross, load_sem.at[2]),
        pltpu.make_async_copy(near_cols, near_at, load_sem.at[3]),
        pltpu.make_async_copy(cross_cols, cross_at, load_sem.at[4]),
    ]

    def beside(step):
        return nearby.at[pl.ds((1 + step) * per, per)]

    own_near = pltpu.make_async_copy(factor, beside(0), own_sem.at[0])

    def rows_of(column):
        return pl.ds(pl.multiple_of(column * width, width), width)

    own_full = pltpu.make_async_copy(factor, full.at[:, rows_of(q), :], own_sem.at[1])

    barrier = pltpu.get_barrier_semaphore()

    def signal(sem, **where):
        pl.semaphore_signal(sem, inc=1, device_id=where, device_id_type=pl.DeviceIdType.MESH)

    greets = [
        (jnp.logical_or(q < col_mate, jnp.logical_and(r == 0, col_mate == 0)), {"col": col_mate}),
        (s == 0, {"rows": mate}),
        (jnp.logical_and(upper == 0, m + 2 < half), {"rows": r + 2}),
        (jnp.logical_and(upper == 0, beyond), {"rows": half + s}),
    ] + [(lower_inmost, {"rows": half + 2 * e + s}) for e in range(planes)]
    greets += [(q < column, {"col": column}) for column in col_cousins]
    late_greets = [(jnp.logical_and(is_upper, m + 2 < half), {"rows": r + 2})]
    heard = [jnp.logical_or(q > col_mate, origin), s == 1, m >= 2, is_upper] + [q > column for column in col_cousins]
    heard += [upper_inmost] * (planes - 1)
    answers = [
        (q > col_mate, CORE, {"col": col_mate}),
        (s == 1, MATE, {"rows": mate}),
        (m >= 2, NEXT, {"rows": r - 2}),
    ] + [(upper_inmost, CROSS, {"rows": half - 2 - 2 * e + s}) for e in range(planes)]
    answers += [(q > column, COUSIN + cousins - 1 - k, {"col": column}) for k, column in enumerate(col_cousins)]

    for condition, where in greets:
        pl.when(condition)(functools.partial(signal, barrier, **where))

    own_full.start()
    own_near.start()
    for load in loads:
        load.start()
    with jax.named_scope("bar"):
        pl.semaphore_wait(barrier, sum(x.astype(jnp.int32) for x in heard))
    for condition, where in late_greets:
        pl.when(condition)(functools.partial(signal, barrier, **where))
    for condition, k, where in answers:
        pl.when(condition)(functools.partial(signal, ready.at[k], **where))

    def send(src, dst, send_sem, recv_sem, **where):
        return pltpu.make_async_remote_copy(
            src_ref=src, dst_ref=dst, send_sem=send_sem, recv_sem=recv_sem,
            device_id=where, device_id_type=pl.DeviceIdType.MESH,
        )

    halves = split(per, col_recv.shape[1])

    def column_piece(column, h):
        return full.at[halves[h], rows_of(column), :]

    def slot(row, p):
        return everyone.at[pl.ds(row * per + cut[p], cut[p + 1] - cut[p])]

    crossing = [
        send(
            factor.at[pl.ds(cut[p], cut[p + 1] - cut[p])], slot(r, p),
            cross_send.at[0], chain_recv.at[d, p], rows=target,
        )
        for p in range(parts)
    ]
    toward = 1 - 2 * s
    to_mate = [send(factor, beside(-toward), near_send.at[0], near_recv.at[0], rows=mate)]
    to_core = [
        send(factor.at[halves[h]], column_piece(q, h), col_send.at[0], col_recv.at[q, h], col=col_mate)
        for h in range(len(halves))
    ]
    to_cousins = [
        [
            send(factor.at[halves[h]], column_piece(q, h), col_send.at[0], col_recv.at[q, h], col=column)
            for h in range(len(halves))
        ]
        for k, column in enumerate(col_cousins)
    ]
    firsts = [(is_upper, None, crossing), (s == 1, MATE, to_mate)]
    firsts += [(q > column, COUSIN + k, to_cousins[k]) for k, column in enumerate(col_cousins)]
    firsts += [(q > col_mate, CORE, to_core)]

    def start_all(copies):
        for copy in copies:
            copy.start()

    with jax.named_scope("own"):
        for condition, _, copies in firsts:
            pl.when(condition)(functools.partial(start_all, copies))

        def after_answer(k, copies):
            pl.semaphore_wait(ready.at[k], 1)
            start_all(copies)

        for condition, k, copies in firsts[:0:-1]:
            pl.when(jnp.logical_not(condition))(functools.partial(after_answer, k, copies))
        pl.when(upper == 0)(functools.partial(after_answer, CROSS, crossing))
        pl.when(m + 2 < half)(lambda: pl.semaphore_wait(ready.at[NEXT], 1))

    sent = [(None, copy) for copy in to_mate]

    def landed(ref, sem):
        send(ref, ref, near_send.at[0], sem, rows=mate).wait_recv()

    def spread(e, p):
        ref = slot(other_row(e, s), p)
        return (
            send(ref, ref, outer_send.at[0], chain_recv.at[e, p], rows=outer),
            send(ref, ref, mate_send.at[0], mate_recv.at[e], rows=mate),
        )

    def forward(e, p):
        landed(slot(other_row(e, s), p), chain_recv.at[e, p])
        on, across = spread(e, p)
        pl.when(has_outer)(on.start)
        across.start()

    def pass_near():
        there = beside(toward)
        landed(there, near_recv.at[0])
        condition = jnp.where(s == 1, m >= 2, m + 2 < half)
        copy = send(there, beside(-toward), near_send.at[1], near_recv.at[1], rows=r + 2 * toward)
        pl.when(condition)(copy.start)
        sent.append((condition, copy))

    def arrive_column(column, h):
        landed(column_piece(column, h), col_recv.at[column, h])

    eye = (
        lax.broadcasted_iota(jnp.int32, (width, order), 0) + q * width
        == lax.broadcasted_iota(jnp.int32, (width, order), 1)
    ).astype(F32)

    def prepare(i, carry):
        z_t = full[i]
        own = full[i, rows_of(q), :]
        square = (-0.5 * dot(z_t, z_t, TN)).astype(BF16)
        blocks = [v_near[i, k] for k in range(near)] + [v_cross[i, k] for k in range(cross)]
        for k in range(near + cross):
            g[i, k] = dot(blocks[k], square, TN).astype(BF16)
        product = dot(own, v_diag[i], NT).astype(BF16)
        residual = (eye - dot(product, z_t, NT)).astype(BF16)
        w_diag[i] = (own.astype(F32) + 0.5 * dot(residual, z_t)).astype(BF16)
        return carry

    def rows_from(e):
        return everyone.at[pl.ds(other_row(e, 1 - s) * per, per)]

    chunks = [(e, p) for e in range(planes) for p in range(parts)]

    def forwards(first, last):
        for e, p in chunks[first:last]:
            with jax.named_scope(f"x{e}{p}"):
                forward(e, p)

    def pass_columns():
        for h in range(len(halves)):
            for k, column in enumerate(col_cousins):
                arrive_column(column, h)
                ref = column_piece(column, h)
                send(ref, ref, col_send.at[0], col_recv.at[column, h], col=col_mate).start()

    first_core = q % 2 == 0
    heads = [
        (jnp.logical_and(first_core, upper == 0), 1),
        (jnp.logical_and(first_core, is_upper), 0),
        (jnp.logical_not(first_core), parts - 1),
    ]

    def take(where, third):
        for condition, head in heads:
            pieces = (chunks[:head], chunks[parts:], chunks[head:parts])

            def some():
                for e, p in pieces[third]:
                    with jax.named_scope(f"x{e}{p}"):
                        forward(e, p)
            if pieces[third]:
                pl.when(jnp.logical_and(where, condition))(some)

    beyond_first = jnp.logical_and(beyond, first_core)
    beyond_second = jnp.logical_and(beyond, jnp.logical_not(first_core))

    def spread_rows(step, first, last):
        with jax.named_scope(f"prep{step}"):
            lax.fori_loop(first, last, prepare, 0, unroll=True)

    take(inmost, 0)
    with jax.named_scope("colf"):
        pass_columns()
    take(inmost, 1)
    take(beyond_second, 0)
    take(inmost, 2)
    with jax.named_scope("loads"):
        own_full.wait()
        for load in loads:
            load.wait()
    with jax.named_scope("cols"):
        for h in range(len(halves)):
            arrive_column(col_mate, h)
            for k in range(1, c // 2):
                arrive_column((col_mate + 2 * k) % c, h)

    row_cut = [per * k // 14 for k in ROW_CUT]
    spread_rows(0, row_cut[0], row_cut[1])
    take(beyond_first, 0)
    take(beyond_second, 1)
    with jax.named_scope("near"):
        pass_near()
    spread_rows(1, row_cut[1], row_cut[2])
    take(beyond_first, 1)
    take(beyond, 2)
    spread_rows(2, row_cut[2], row_cut[3])

    with jax.named_scope("nwait"):
        own_near.wait()
        within = jnp.logical_and(m - toward >= 0, m - toward < half)
        edge = jnp.logical_and(jnp.logical_not(within), jnp.logical_and(r - toward >= 0, r - toward < n))
        pl.when(within)(functools.partial(landed, beside(-toward), near_recv.at[1]))

        @pl.when(edge)
        def _():
            landed(rows_from(0), mate_recv.at[0])
            copy = pltpu.make_async_copy(everyone.at[pl.ds((r - toward) * per, per)], beside(-toward), edge_sem.at[0])
            copy.start()
            copy.wait()

    base = (r - 1) * per

    def finish_near(i, carry):
        for k in range(near):
            place = jnp.clip(near_at[k, i] - base, 0, 3 * per - 1)
            w_near[i, k] = dot(nearby[place], g[i, k]).astype(BF16)
        return carry

    def finish_cross(i, carry):
        for k in range(cross):
            w_cross[i, k] = dot(everyone[cross_at[k, i]], g[i, near + k]).astype(BF16)
        return carry

    with jax.named_scope("ndots"):
        lax.fori_loop(0, per, finish_near, 0, unroll=True)
    with jax.named_scope("fin"):
        pl.when(jnp.logical_not(edge))(functools.partial(landed, rows_from(0), mate_recv.at[0]))
        for e in range(1, planes):
            landed(rows_from(e), mate_recv.at[e])
    with jax.named_scope("cdots"):
        lax.fori_loop(0, per, finish_cross, 0, unroll=True)
    with jax.named_scope("sends"):
        def gone(ref, sem):
            send(ref, ref, sem, near_recv.at[0], rows=mate).wait_send()

        gone(everyone.at[pl.ds(0, planes * per)], mate_send.at[0])
        pl.when(has_outer)(functools.partial(gone, everyone.at[pl.ds(0, planes * per)], outer_send.at[0]))
        gone(everyone.at[pl.ds(0, per)], cross_send.at[0])
        gone(everyone.at[pl.ds(0, per * (2 * cousins + 1))], col_send.at[0])
        for condition, copy in sent:
            if condition is None:
                copy.wait_send()
            else:
                pl.when(condition)(copy.wait_send)


def store_kernel(w_diag, w_near, w_cross, o_diag, o_near, o_cross, sem):
    copies = [
        pltpu.make_async_copy(w_diag, o_diag, sem.at[0]),
        pltpu.make_async_copy(w_near, o_near, sem.at[1]),
        pltpu.make_async_copy(w_cross, o_cross, sem.at[2]),
    ]
    for copy in copies:
        copy.start()
    for copy in copies:
        copy.wait()


def body(n, c, factor_t, intersection_diag, intersection_near, intersection_cross, near_cols, cross_cols):
    per, width, order = factor_t.shape
    near, cross = near_cols.shape[1], cross_cols.shape[1]
    planes = n // 4
    parts = max(1, min(PARTS // planes, per))
    col_parts = 2 if per % 2 == 0 else 1
    smem = pltpu.SMEM
    vmem = pl.BlockSpec(memory_space=pltpu.VMEM)
    hbm = pl.BlockSpec(memory_space=pl.ANY)
    dma = pltpu.SemaphoreType.DMA
    shapes = ((per, width, order), (per, near, width, order), (per, cross, width, order))
    kept = 2 * order * width * per * (1 + near + cross)
    results = pl.pallas_call(
        functools.partial(refine_kernel, n, c, parts),
        out_shape=tuple(pltpu.VMEM(shape, BF16) for shape in shapes),
        in_specs=[pl.BlockSpec(memory_space=pltpu.HBM)] * 6,
        out_specs=(vmem,) * 3,
        scratch_shapes=[
            pltpu.VMEM((n * per, width, order), BF16),
            pltpu.VMEM((3 * per, width, order), BF16),
            pltpu.VMEM((per, near + cross, order, order), BF16),
            pltpu.VMEM((per, order, order), BF16),
            pltpu.VMEM(intersection_diag.shape, BF16),
            pltpu.VMEM(intersection_near.shape, BF16),
            pltpu.VMEM(intersection_cross.shape, BF16),
            smem((near, per), jnp.int32),
            smem((cross, per), jnp.int32),
            dma((5,)),
            dma((2,)),
            dma((1,)),
            dma((1,)),
            dma((c, col_parts)),
            dma((2,)),
            dma((2,)),
            dma((1,)),
            dma((1,)),
            dma((1,)),
            dma((planes, parts)),
            dma((planes,)),
            pltpu.SemaphoreType.REGULAR((3 + c // 2,)),
        ],
        compiler_params=pltpu.CompilerParams(
            collective_id=0, has_side_effects=True, vmem_limit_bytes=VMEM_ALL - kept - SLACK,
        ),
    )(factor_t, intersection_diag, intersection_near, intersection_cross, near_cols.T, cross_cols.T)
    return pl.pallas_call(
        store_kernel,
        out_shape=tuple(jax.ShapeDtypeStruct(shape, BF16) for shape in shapes),
        in_specs=[vmem] * 3,
        out_specs=(hbm,) * 3,
        scratch_shapes=[dma((3,))],
        compiler_params=pltpu.CompilerParams(vmem_limit_bytes=VMEM_LIMIT),
    )(*results)


def solution(mesh):
    placed = (
        P("rows", "col", None),
        P("rows", None, None),
        P("rows", None, None, None),
        P("rows", None, None, None),
        P("rows", None),
        P("rows", None),
    )
    return jax.shard_map(
        functools.partial(body, mesh.shape["rows"], mesh.shape["col"]),
        mesh=mesh,
        in_specs=placed,
        out_specs=(
            P("rows", "col", None),
            P("rows", None, "col", None),
            P("rows", None, "col", None),
        ),
        check_vma=False,
    )
```

time: 23.4 us -> 19.6 us (0.84)
  Pallas kernels: 22.5 us -> 18.8 us
    pallas_call x2, Pallas kernels: 22.5 us -> 18.8 us  [the longest x1 17.8 us: body(): pl.pallas_call(functools.partial(refine_kernel, n, c, parts), out_shape=t...]
where the time goes in v1:
time: 19.6 us; the launch traced here: 19.4 us
  Pallas kernels  18.8 us (96%)
  between operations  0.64 us (3%)
    pallas_call x1, Pallas kernels, body(): pl.pallas_call(functools.partial(refine_kernel, n, c, parts), out_shape=t...  17.8 us
    pallas_call x1, Pallas kernels, body(): pl.pallas_call(store_kernel, out_shape=tuple((jax.ShapeDtypeStruct(shape,...  0.95 us

profile of v1, /device:TPU:0, one launch (start us, length us, event | category | flops | bytes accessed | tf_op | source)
XLA Modules:
  0.0 19.4 jit_solution(6207533349143480551)
XLA Ops:
  0.6 17.8 %shard_map.85 = (bf16[14,32,128]{2,1,0:T(8,128)(2,1)S(1)}, bf16[14,3,32,128]{3,2,1,0:T(8,128)(2,1)S(1)}, bf16[14,4,32,128]{3,2,1,0:T(8,128)(2,1)S(1)}) custom-call(bf16[14,32,128]{2,1,0:T(8,128)(2,1)} %factor.1, bf16[14,128,128]{2,1,0:T(8,128)(2,1)} %s_diag.1, bf16[14,3,128,128]{3,2,1,0:T(8,128)(2,1)} %s_near.1, bf16[14,4,128,128]{3,2,1,0:T(8,128)(2,1)} %s_cross.1, ...), custom_call_target="tpu_custom_call" | custom-call | tf_op jit(solution)/shard_map/pallas_call | solution.py:364
  18.5 0.9 %shard_map.86 = (bf16[14,32,128]{2,1,0:T(8,128)(2,1)}, bf16[14,3,32,128]{3,2,1,0:T(8,128)(2,1)}, bf16[14,4,32,128]{3,2,1,0:T(8,128)(2,1)}) custom-call(bf16[14,32,128]{2,1,0:T(8,128)(2,1)S(1)} %get-tuple-element.6.w_diag, bf16[14,3,32,128]{3,2,1,0:T(8,128)(2,1)S(1)} %get-tuple-element.7.w_near, bf16[14,4,32,128]{3,2,1,0:T(8,128)(2,1)S(1)} %get-tuple-element.8.w_cross), custom_call_target="tpu_custom_call" | custom-call | tf_op jit(solution)/shard_map/pallas_call | solution.py:397

commit v2 on v1

--- a/solution.py
+++ b/solution.py
@@ -9,8 +9,8 @@
 
 F32 = jnp.float32
 BF16 = jnp.bfloat16
-PARTS = 8
-ROW_CUT = (0, 4, 8, 14)
+PARTS = 14
+ROW_CUT = (0, 5, 10, 14)
 VMEM_LIMIT = 16 * 1024 * 1024
 VMEM_ALL = 67043328
 SLACK = 96 * 1024
@@ -33,7 +33,7 @@
     w_diag, w_near, w_cross,
     everyone, nearby, g, full, v_diag, v_near, v_cross, near_at, cross_at,
     load_sem, own_sem, edge_sem, col_send, col_recv, near_send, near_recv,
-    cross_send, outer_send, mate_send, chain_recv, mate_recv, ready,
+    cross_send, outer_send, mate_send, slant_send, chain_recv, mate_recv, ready,
 ):
     per, width, order = factor.shape
     near, cross = v_near.shape[1], v_cross.shape[1]
@@ -52,6 +52,7 @@
     lower_inmost = jnp.logical_and(upper == 0, inmost)
     upper_inmost = jnp.logical_and(is_upper, inmost)
     has_outer = d + 1 < planes
+    first_core = q % 2 == 0
     mate = r + 1 - 2 * s
     target = jnp.where(is_upper, half - 2 + s, half + s)
     outer = jnp.where(is_upper, r + 2, r - 2)
@@ -191,13 +192,31 @@
         pl.when(has_outer)(on.start)
         across.start()
 
-    def pass_near():
-        there = beside(toward)
-        landed(there, near_recv.at[0])
-        condition = jnp.where(s == 1, m >= 2, m + 2 < half)
-        copy = send(there, beside(-toward), near_send.at[1], near_recv.at[1], rows=r + 2 * toward)
-        pl.when(condition)(copy.start)
-        sent.append((condition, copy))
+    slant = jnp.logical_and(jnp.logical_and(lower_inmost, has_outer), s == 1)
+    slanted = jnp.logical_and(jnp.logical_and(upper == 0, d == 1), s == 1)
+
+    def forward_last(e, p):
+        ref = slot(other_row(e, s), p)
+        landed(ref, chain_recv.at[e, p])
+        on, across = spread(e, p)
+        aslant = send(ref, ref, slant_send.at[0], mate_recv.at[e], rows=outer - 1)
+        pl.when(slant)(aslant.start)
+        pl.when(jnp.logical_and(has_outer, jnp.logical_not(slant)))(on.start)
+        pl.when(jnp.logical_not(slanted))(across.start)
+
+    def near_copy(src_ref, step, row):
+        return send(src_ref, beside(step), near_send.at[1], near_recv.at[1], rows=row)
+
+    passing = near_copy(beside(toward), -toward, r + 2 * toward)
+    prompt = jnp.logical_and(lower_inmost, first_core)
+    passes = jnp.logical_and(jnp.where(s == 1, m >= 2, m + 2 < half), jnp.logical_not(jnp.logical_and(prompt, s == 1)))
+    direct = near_copy(factor, 1, r - 1)
+    directs = jnp.logical_and(jnp.logical_and(prompt, s == 0), m >= 2)
+    sent += [(passes, passing), (directs, direct)]
+
+    def pass_near(where):
+        pl.when(jnp.logical_and(where, passes))(passing.start)
+        pl.when(jnp.logical_and(where, directs))(direct.start)
 
     def arrive_column(column, h):
         landed(column_piece(column, h), col_recv.at[column, h])
@@ -212,8 +231,9 @@
         own = full[i, rows_of(q), :]
         square = (-0.5 * dot(z_t, z_t, TN)).astype(BF16)
         blocks = [v_near[i, k] for k in range(near)] + [v_cross[i, k] for k in range(cross)]
+        tall = dot(jnp.concatenate(blocks, axis=1), square, TN).astype(BF16)
         for k in range(near + cross):
-            g[i, k] = dot(blocks[k], square, TN).astype(BF16)
+            g[i, k] = tall[k * order:(k + 1) * order]
         product = dot(own, v_diag[i], NT).astype(BF16)
         residual = (eye - dot(product, z_t, NT)).astype(BF16)
         w_diag[i] = (own.astype(F32) + 0.5 * dot(residual, z_t)).astype(BF16)
@@ -236,23 +256,36 @@
                 ref = column_piece(column, h)
                 send(ref, ref, col_send.at[0], col_recv.at[column, h], col=col_mate).start()
 
-    first_core = q % 2 == 0
     heads = [
         (jnp.logical_and(first_core, upper == 0), 1),
         (jnp.logical_and(first_core, is_upper), 0),
-        (jnp.logical_not(first_core), parts - 1),
-    ]
-
-    def take(where, third):
+        (jnp.logical_not(first_core), max(1, parts * 3 // 4)),
+    ]
+
+    middle = len(chunks) - parts - parts // 2
+
+    def pieces_of(head):
+        passing = chunks[parts:]
+        return chunks[:head], passing[:middle], passing[middle:], chunks[head:parts]
+
+    def aslant_from(head):
+        return 2 if head == 1 else 3
+
+    def take(where, *places):
         for condition, head in heads:
-            pieces = (chunks[:head], chunks[parts:], chunks[head:parts])
-
             def some():
-                for e, p in pieces[third]:
-                    with jax.named_scope(f"x{e}{p}"):
-                        forward(e, p)
-            if pieces[third]:
-                pl.when(jnp.logical_and(where, condition))(some)
+                last = []
+                for place in places:
+                    for e, p in pieces_of(head)[place]:
+                        with jax.named_scope(f"x{e}{p}"):
+                            if place < aslant_from(head):
+                                forward(e, p)
+                            else:
+                                forward_last(e, p)
+                                last.append(spread(e, p)[0])
+                if last:
+                    pl.when(slant)(functools.partial(start_all, last))
+            pl.when(jnp.logical_and(where, condition))(some)
 
     beyond_first = jnp.logical_and(beyond, first_core)
     beyond_second = jnp.logical_and(beyond, jnp.logical_not(first_core))
@@ -266,7 +299,10 @@
         pass_columns()
     take(inmost, 1)
     take(beyond_second, 0)
-    take(inmost, 2)
+    with jax.named_scope("mate"):
+        landed(beside(toward), near_recv.at[0])
+    take(inmost, 2, 3)
+    pass_near(prompt)
     with jax.named_scope("loads"):
         own_full.wait()
         for load in loads:
@@ -280,13 +316,18 @@
     row_cut = [per * k // 14 for k in ROW_CUT]
     spread_rows(0, row_cut[0], row_cut[1])
     take(beyond_first, 0)
-    take(beyond_second, 1)
+    take(beyond_second, 1, 2)
     with jax.named_scope("near"):
-        pass_near()
+        pass_near(jnp.logical_not(lower_inmost))
     spread_rows(1, row_cut[1], row_cut[2])
+    pass_near(jnp.logical_and(lower_inmost, jnp.logical_not(first_core)))
+    passes_on = jnp.logical_and(beyond, jnp.logical_not(slanted))
     take(beyond_first, 1)
-    take(beyond, 2)
+    take(jnp.logical_and(passes_on, first_core), 2)
+    take(passes_on, 3)
     spread_rows(2, row_cut[2], row_cut[3])
+    take(jnp.logical_and(slanted, first_core), 2)
+    take(slanted, 3)
 
     with jax.named_scope("nwait"):
         own_near.wait()
@@ -326,7 +367,16 @@
         def gone(ref, sem):
             send(ref, ref, sem, near_recv.at[0], rows=mate).wait_send()
 
-        gone(everyone.at[pl.ds(0, planes * per)], mate_send.at[0])
+        pl.when(jnp.logical_not(slanted))(functools.partial(gone, everyone.at[pl.ds(0, planes * per)], mate_send.at[0]))
+        for condition, head in heads:
+            last = sum(cut[p + 1] - cut[p] for piece in pieces_of(head)[aslant_from(head):] for e, p in piece)
+            pl.when(jnp.logical_and(slanted, condition))(
+                functools.partial(gone, everyone.at[pl.ds(0, planes * per - last)], mate_send.at[0])
+            )
+            if last:
+                pl.when(jnp.logical_and(slant, condition))(
+                    functools.partial(gone, everyone.at[pl.ds(0, last)], slant_send.at[0])
+                )
         pl.when(has_outer)(functools.partial(gone, everyone.at[pl.ds(0, planes * per)], outer_send.at[0]))
         gone(everyone.at[pl.ds(0, per)], cross_send.at[0])
         gone(everyone.at[pl.ds(0, per * (2 * cousins + 1))], col_send.at[0])
@@ -386,6 +436,7 @@
             dma((1,)),
             dma((1,)),
             dma((1,)),
+            dma((1,)),
             dma((planes, parts)),
             dma((planes,)),
             pltpu.SemaphoreType.REGULAR((3 + c // 2,)),

time: 19.6 us -> 18.6 us (0.949)
  Pallas kernels: 18.8 us -> 17.8 us
    pallas_call x1, Pallas kernels: 17.8 us -> 16.9 us  [body(): pl.pallas_call(functools.partial(refine_kernel, n, c, parts), out_shape=t...]
where the time goes in v2:
time: 18.6 us; the launch traced here: 18.5 us
  Pallas kernels  17.8 us (96%)
  between operations  0.64 us (3%)
    pallas_call x1, Pallas kernels, body(): pl.pallas_call(functools.partial(refine_kernel, n, c, parts), out_shape=t...  16.9 us
    pallas_call x1, Pallas kernels, body(): pl.pallas_call(store_kernel, out_shape=tuple((jax.ShapeDtypeStruct(shape,...  0.95 us

profile of v2, /device:TPU:0, one launch (start us, length us, event | category | flops | bytes accessed | tf_op | source)
XLA Modules:
  0.0 18.5 jit_solution(17380760213876853525)
XLA Ops:
  0.6 16.9 %shard_map.85 = (bf16[14,32,128]{2,1,0:T(8,128)(2,1)S(1)}, bf16[14,3,32,128]{3,2,1,0:T(8,128)(2,1)S(1)}, bf16[14,4,32,128]{3,2,1,0:T(8,128)(2,1)S(1)}) custom-call(bf16[14,32,128]{2,1,0:T(8,128)(2,1)} %factor.1, bf16[14,128,128]{2,1,0:T(8,128)(2,1)} %s_diag.1, bf16[14,3,128,128]{3,2,1,0:T(8,128)(2,1)} %s_near.1, bf16[14,4,128,128]{3,2,1,0:T(8,128)(2,1)} %s_cross.1, ...), custom_call_target="tpu_custom_call" | custom-call | tf_op jit(solution)/shard_map/pallas_call | solution.py:414
  17.5 0.9 %shard_map.86 = (bf16[14,32,128]{2,1,0:T(8,128)(2,1)}, bf16[14,3,32,128]{3,2,1,0:T(8,128)(2,1)}, bf16[14,4,32,128]{3,2,1,0:T(8,128)(2,1)}) custom-call(bf16[14,32,128]{2,1,0:T(8,128)(2,1)S(1)} %get-tuple-element.6.w_diag, bf16[14,3,32,128]{3,2,1,0:T(8,128)(2,1)S(1)} %get-tuple-element.7.w_near, bf16[14,4,32,128]{3,2,1,0:T(8,128)(2,1)S(1)} %get-tuple-element.8.w_cross), custom_call_target="tpu_custom_call" | custom-call | tf_op jit(solution)/shard_map/pallas_call | solution.py:448

commit v3 on v2

--- a/solution.py
+++ b/solution.py
@@ -60,7 +60,7 @@
     col_cousins = [(q + 2 * k) % c for k in range(1, c // 2)]
     cousins = len(col_cousins)
     origin = jnp.logical_and(r == 0, q == 0)
-    CORE, MATE, NEXT, CROSS, COUSIN = 0, 1, 2, 3, 4
+    CORE, MATE, NEXT, CROSS, SLANT, COUSIN = 0, 1, 2, 3, 4, 5
 
     def other_row(e, side):
         return jnp.where(is_upper, half - 2 - 2 * e, half + 2 * e) + side
@@ -171,6 +171,9 @@
 
         for condition, k, copies in firsts[:0:-1]:
             pl.when(jnp.logical_not(condition))(functools.partial(after_answer, k, copies))
+        pl.when(jnp.logical_and(jnp.logical_and(lower_inmost, has_outer), s == 0))(
+            functools.partial(signal, ready.at[SLANT], rows=mate)
+        )
         pl.when(upper == 0)(functools.partial(after_answer, CROSS, crossing))
         pl.when(m + 2 < half)(lambda: pl.semaphore_wait(ready.at[NEXT], 1))
 
@@ -262,7 +265,7 @@
         (jnp.logical_not(first_core), max(1, parts * 3 // 4)),
     ]
 
-    middle = len(chunks) - parts - parts // 2
+    middle = len(chunks) - parts - (parts * 3 // 4)
 
     def pieces_of(head):
         passing = chunks[parts:]
@@ -299,8 +302,7 @@
         pass_columns()
     take(inmost, 1)
     take(beyond_second, 0)
-    with jax.named_scope("mate"):
-        landed(beside(toward), near_recv.at[0])
+    pl.when(slant)(lambda: pl.semaphore_wait(ready.at[SLANT], 1))
     take(inmost, 2, 3)
     pass_near(prompt)
     with jax.named_scope("loads"):
@@ -318,16 +320,14 @@
     take(beyond_first, 0)
     take(beyond_second, 1, 2)
     with jax.named_scope("near"):
-        pass_near(jnp.logical_not(lower_inmost))
+        landed(beside(toward), near_recv.at[0])
+        pass_near(jnp.logical_not(prompt))
     spread_rows(1, row_cut[1], row_cut[2])
-    pass_near(jnp.logical_and(lower_inmost, jnp.logical_not(first_core)))
     passes_on = jnp.logical_and(beyond, jnp.logical_not(slanted))
     take(beyond_first, 1)
     take(jnp.logical_and(passes_on, first_core), 2)
     take(passes_on, 3)
     spread_rows(2, row_cut[2], row_cut[3])
-    take(jnp.logical_and(slanted, first_core), 2)
-    take(slanted, 3)
 
     with jax.named_scope("nwait"):
         own_near.wait()
@@ -357,6 +357,8 @@
 
     with jax.named_scope("ndots"):
         lax.fori_loop(0, per, finish_near, 0, unroll=True)
+    take(jnp.logical_and(slanted, first_core), 2)
+    take(slanted, 3)
     with jax.named_scope("fin"):
         pl.when(jnp.logical_not(edge))(functools.partial(landed, rows_from(0), mate_recv.at[0]))
         for e in range(1, planes):
@@ -439,7 +441,7 @@
             dma((1,)),
             dma((planes, parts)),
             dma((planes,)),
-            pltpu.SemaphoreType.REGULAR((3 + c // 2,)),
+            pltpu.SemaphoreType.REGULAR((4 + c // 2,)),
         ],
         compiler_params=pltpu.CompilerParams(
             collective_id=0, has_side_effects=True, vmem_limit_bytes=VMEM_ALL - kept - SLACK,

time: 18.6 us -> 18 us (0.968)
  Pallas kernels: 17.8 us -> 17.1 us
    pallas_call x1, Pallas kernels: 16.9 us -> 16.1 us  [body(): pl.pallas_call(functools.partial(refine_kernel, n, c, parts), out_shape=t...]
where the time goes in v3:
time: 18 us; the launch traced here: 17.7 us
  Pallas kernels  17.1 us (95%)
  between operations  0.64 us (4%)
    pallas_call x1, Pallas kernels, body(): pl.pallas_call(functools.partial(refine_kernel, n, c, parts), out_shape=t...  16.1 us
    pallas_call x1, Pallas kernels, body(): pl.pallas_call(store_kernel, out_shape=tuple((jax.ShapeDtypeStruct(shape,...  0.95 us

profile of v3, /device:TPU:0, one launch (start us, length us, event | category | flops | bytes accessed | tf_op | source)
XLA Modules:
  0.0 17.7 jit_solution(18151219059059534786)
XLA Ops:
  0.6 16.1 %shard_map.85 = (bf16[14,32,128]{2,1,0:T(8,128)(2,1)S(1)}, bf16[14,3,32,128]{3,2,1,0:T(8,128)(2,1)S(1)}, bf16[14,4,32,128]{3,2,1,0:T(8,128)(2,1)S(1)}) custom-call(bf16[14,32,128]{2,1,0:T(8,128)(2,1)} %factor.1, bf16[14,128,128]{2,1,0:T(8,128)(2,1)} %s_diag.1, bf16[14,3,128,128]{3,2,1,0:T(8,128)(2,1)} %s_near.1, bf16[14,4,128,128]{3,2,1,0:T(8,128)(2,1)} %s_cross.1, ...), custom_call_target="tpu_custom_call" | custom-call | tf_op jit(solution)/shard_map/pallas_call | solution.py:416
  16.8 0.9 %shard_map.86 = (bf16[14,32,128]{2,1,0:T(8,128)(2,1)}, bf16[14,3,32,128]{3,2,1,0:T(8,128)(2,1)}, bf16[14,4,32,128]{3,2,1,0:T(8,128)(2,1)}) custom-call(bf16[14,32,128]{2,1,0:T(8,128)(2,1)S(1)} %get-tuple-element.6.w_diag, bf16[14,3,32,128]{3,2,1,0:T(8,128)(2,1)S(1)} %get-tuple-element.7.w_near, bf16[14,4,32,128]{3,2,1,0:T(8,128)(2,1)S(1)} %get-tuple-element.8.w_cross), custom_call_target="tpu_custom_call" | custom-call | tf_op jit(solution)/shard_map/pallas_call | solution.py:450

commit v4 on v3

--- a/solution.py
+++ b/solution.py
@@ -32,7 +32,7 @@
     factor, s_diag, s_near, s_cross, near_cols, cross_cols,
     w_diag, w_near, w_cross,
     everyone, nearby, g, full, v_diag, v_near, v_cross, near_at, cross_at,
-    load_sem, own_sem, edge_sem, col_send, col_recv, near_send, near_recv,
+    load_sem, own_sem, col_send, col_recv, near_send, near_recv,
     cross_send, outer_send, mate_send, slant_send, chain_recv, mate_recv, ready,
 ):
     per, width, order = factor.shape
@@ -338,7 +338,7 @@
         @pl.when(edge)
         def _():
             landed(rows_from(0), mate_recv.at[0])
-            copy = pltpu.make_async_copy(everyone.at[pl.ds((r - toward) * per, per)], beside(-toward), edge_sem.at[0])
+            copy = pltpu.make_async_copy(everyone.at[pl.ds((r - toward) * per, per)], beside(-toward), own_sem.at[0])
             copy.start()
             copy.wait()
 
@@ -406,7 +406,7 @@
     near, cross = near_cols.shape[1], cross_cols.shape[1]
     planes = n // 4
     parts = max(1, min(PARTS // planes, per))
-    col_parts = 2 if per % 2 == 0 else 1
+    col_parts = 1
     smem = pltpu.SMEM
     vmem = pl.BlockSpec(memory_space=pltpu.VMEM)
     hbm = pl.BlockSpec(memory_space=pl.ANY)
@@ -431,7 +431,6 @@
             dma((5,)),
             dma((2,)),
             dma((1,)),
-            dma((1,)),
             dma((c, col_parts)),
             dma((2,)),
             dma((2,)),

time: 18 us -> 18 us (level)
  no operation moved by 1% of the time
where the time goes in v4:
time: 18 us; the launch traced here: 17.7 us
  Pallas kernels  17 us (94%)
  between operations  0.64 us (4%)
    pallas_call x1, Pallas kernels, body(): pl.pallas_call(functools.partial(refine_kernel, n, c, parts), out_shape=t...  16.1 us
    pallas_call x1, Pallas kernels, body(): pl.pallas_call(store_kernel, out_shape=tuple((jax.ShapeDtypeStruct(shape,...  0.95 us

profile of v4, /device:TPU:0, one launch (start us, length us, event | category | flops | bytes accessed | tf_op | source)
XLA Modules:
  0.0 17.7 jit_solution(17242933866624748540)
XLA Ops:
  0.6 16.1 %shard_map.85 = (bf16[14,32,128]{2,1,0:T(8,128)(2,1)S(1)}, bf16[14,3,32,128]{3,2,1,0:T(8,128)(2,1)S(1)}, bf16[14,4,32,128]{3,2,1,0:T(8,128)(2,1)S(1)}) custom-call(bf16[14,32,128]{2,1,0:T(8,128)(2,1)} %factor.1, bf16[14,128,128]{2,1,0:T(8,128)(2,1)} %s_diag.1, bf16[14,3,128,128]{3,2,1,0:T(8,128)(2,1)} %s_near.1, bf16[14,4,128,128]{3,2,1,0:T(8,128)(2,1)} %s_cross.1, ...), custom_call_target="tpu_custom_call" | custom-call | tf_op jit(solution)/shard_map/pallas_call | solution.py:416
  16.7 0.9 %shard_map.86 = (bf16[14,32,128]{2,1,0:T(8,128)(2,1)}, bf16[14,3,32,128]{3,2,1,0:T(8,128)(2,1)}, bf16[14,4,32,128]{3,2,1,0:T(8,128)(2,1)}) custom-call(bf16[14,32,128]{2,1,0:T(8,128)(2,1)S(1)} %get-tuple-element.6.w_diag, bf16[14,3,32,128]{3,2,1,0:T(8,128)(2,1)S(1)} %get-tuple-element.7.w_near, bf16[14,4,32,128]{3,2,1,0:T(8,128)(2,1)S(1)} %get-tuple-element.8.w_cross), custom_call_target="tpu_custom_call" | custom-call | tf_op jit(solution)/shard_map/pallas_call | solution.py:449

commit v5 on v4

--- a/solution.py
+++ b/solution.py
@@ -265,7 +265,7 @@
         (jnp.logical_not(first_core), max(1, parts * 3 // 4)),
     ]
 
-    middle = len(chunks) - parts - (parts * 3 // 4)
+    middle = len(chunks) - parts - (parts * 3 // 5)
 
     def pieces_of(head):
         passing = chunks[parts:]

time: 18 us -> 18.2 us (1.011)
  Pallas kernels: 17 us -> 17.4 us
    pallas_call x1, Pallas kernels: 16.1 us -> 16.4 us  [body(): pl.pallas_call(functools.partial(refine_kernel, n, c, parts), out_shape=t...]
where the time goes in v5:
time: 18.2 us; the launch traced here: 18 us
  Pallas kernels  17.4 us (96%)
  between operations  0.64 us (4%)
    pallas_call x1, Pallas kernels, body(): pl.pallas_call(functools.partial(refine_kernel, n, c, parts), out_shape=t...  16.4 us
    pallas_call x1, Pallas kernels, body(): pl.pallas_call(store_kernel, out_shape=tuple((jax.ShapeDtypeStruct(shape,...  0.95 us

profile of v5, /device:TPU:0, one launch (start us, length us, event | category | flops | bytes accessed | tf_op | source)
XLA Modules:
  0.0 18.0 jit_solution(12556034270624779427)
XLA Ops:
  0.6 16.4 %shard_map.85 = (bf16[14,32,128]{2,1,0:T(8,128)(2,1)S(1)}, bf16[14,3,32,128]{3,2,1,0:T(8,128)(2,1)S(1)}, bf16[14,4,32,128]{3,2,1,0:T(8,128)(2,1)S(1)}) custom-call(bf16[14,32,128]{2,1,0:T(8,128)(2,1)} %factor.1, bf16[14,128,128]{2,1,0:T(8,128)(2,1)} %s_diag.1, bf16[14,3,128,128]{3,2,1,0:T(8,128)(2,1)} %s_near.1, bf16[14,4,128,128]{3,2,1,0:T(8,128)(2,1)} %s_cross.1, ...), custom_call_target="tpu_custom_call" | custom-call | tf_op jit(solution)/shard_map/pallas_call | solution.py:416
  17.1 0.9 %shard_map.86 = (bf16[14,32,128]{2,1,0:T(8,128)(2,1)}, bf16[14,3,32,128]{3,2,1,0:T(8,128)(2,1)}, bf16[14,4,32,128]{3,2,1,0:T(8,128)(2,1)}) custom-call(bf16[14,32,128]{2,1,0:T(8,128)(2,1)S(1)} %get-tuple-element.6.w_diag, bf16[14,3,32,128]{3,2,1,0:T(8,128)(2,1)S(1)} %get-tuple-element.7.w_near, bf16[14,4,32,128]{3,2,1,0:T(8,128)(2,1)S(1)} %get-tuple-element.8.w_cross), custom_call_target="tpu_custom_call" | custom-call | tf_op jit(solution)/shard_map/pallas_call | solution.py:449
